TPU v7x, 32 devices: a whole 2x2x4 slice. The times are simulated.
32 devices in a mesh: ctx: 8 (over z, x), tp: 4 (over y, core).
Axes of the slice: x: 2, y: 2, z: 4, core: 2. Of those that a mesh axis runs over, the one named last changes fastest.
Arguments:
- lin_q: bfloat16 [2048, 4096], P('ctx', 'tp'), may hold values from -6 to 6
- lin_k: bfloat16 [2048, 4096], P('ctx', 'tp'), may hold values from -6 to 6
- lin_v: bfloat16 [2048, 4096], P('ctx', 'tp'), may hold values from -20 to 20
- att_q: bfloat16 [2048, 4096], P('ctx', 'tp'), may hold values from -150 to 150
- att_k: bfloat16 [2048, 1024], P('ctx', 'tp'), may hold values from -7 to 7
- att_v: bfloat16 [2048, 1024], P('ctx', 'tp'), may hold values from -20 to 20
- block_lists: int32 [16, 4], P('ctx'), may hold values from -1 to 15, as said below
- gain_lin: bfloat16 [4096], P('tp'), may hold values from 0.25 to 1.75
- gain_att: bfloat16 [4096], P('tp'), may hold values from 0.25 to 1.75
Outputs:
- mixed: bfloat16 [2048, 4096], P('ctx', 'tp')
Inputs may be any that keep to these rules, and one draw needn't show every extreme that they name: `block_lists`: row b: entry 0 is b; every other entry is either -1 (unused) or a block in b - 4 to b - 1, with no block twice; some row has all 4 entries in use.
All inputs are finite; a program needn't handle non-finite values.
Results may differ from a plain program's by a relative error of at most 0.0049.
Values may be sent and summed in bfloat16 or wider, within the bound.
A program may use at most 192 MiB of HBM per device.

v0:
```python
import jax
import jax.numpy as jnp
from jax import lax
from jax.sharding import PartitionSpec as P

HD = 128
BLK = 128
SPAN = 5


epsilon = 1e-06


def prefix_2(x, axis, combine, identity):
    length, position = (lax.axis_size(axis), lax.axis_index(axis))
    everything = lax.all_gather(x, axis)
    start = jnp.broadcast_to(jnp.asarray(identity, x.dtype), x.shape)

    def step(k, before):
        reached = k < position
        new = combine(before, everything[k])
        return jnp.where(reached, new, before)

    return lax.fori_loop(0, length, step, start)


def from_behind(block, axis, distance):
    devices = range(lax.axis_size(axis))
    route = [(i - distance, i) for i in devices if i - distance in devices]
    return lax.ppermute(block, axis, route)


def add_states(earlier, later):
    return earlier + later


def linear_mixer(lin_q, lin_k, lin_v):
    tokens_here = lin_q.shape[0]
    per_dev = tokens_here // BLK
    heads_local = lin_q.shape[1] // HD
    queries = lin_q.reshape(per_dev, BLK, heads_local, HD)
    keys_here = lin_k.reshape(per_dev, BLK, heads_local, HD)
    values_here = lin_v.reshape(per_dev, BLK, heads_local, HD)
    block_states = jnp.einsum(
        "bshd,bshe->bhde", keys_here, values_here, preferred_element_type=jnp.float32
    )
    device_total = jnp.sum(block_states, axis=0)
    prefix = prefix_2(device_total, "ctx", add_states, jnp.zeros_like(device_total))
    lower = jnp.arange(BLK)[:, None] >= jnp.arange(BLK)[None, :]
    scores = jnp.einsum("bthd,bshd->bhts", queries, keys_here, preferred_element_type=jnp.float32)
    scores = jnp.where(lower[None, None], scores, 0.0).astype(jnp.bfloat16)
    intra = jnp.einsum("bhts,bshd->bthd", scores, values_here, preferred_element_type=jnp.float32)
    running = jnp.cumsum(block_states, axis=0)
    earlier_local = jnp.concatenate([jnp.zeros_like(block_states[:1]), running[:-1]], axis=0)
    carried_low = (prefix[None] + earlier_local).astype(jnp.bfloat16)
    inter = jnp.einsum("bthd,bhde->bthe", queries, carried_low, preferred_element_type=jnp.float32)
    return (intra + inter).reshape(tokens_here, heads_local * HD)


def tree_attention(att_q, att_k, att_v, block_lists):
    tokens_here = att_q.shape[0]
    per_dev = tokens_here // BLK
    kv_local = att_k.shape[1] // HD
    heads_local = att_q.shape[1] // HD
    groups = heads_local // kv_local
    reach_dev = (SPAN - 2) // per_dev + 1
    score_scale = HD ** (-0.5)
    paired = jnp.stack([att_k, att_v])
    pieces = [paired]
    for offset in range(1, reach_dev + 1):
        pieces = [from_behind(paired, "ctx", offset)] + pieces
    window = jnp.concatenate(pieces, axis=1)
    position = lax.axis_index("ctx")
    first_blk = (position - reach_dev) * per_dev

    def one_block(local_blk):
        start_blk = reach_dev * per_dev + local_blk - (SPAN - 1)
        queries = lax.dynamic_slice_in_dim(att_q, local_blk * BLK, BLK, 0).reshape(
            BLK, kv_local, groups, HD
        )
        slab = lax.dynamic_slice_in_dim(window, start_blk * BLK, SPAN * BLK, 1)
        slab_keys = slab[0].reshape(SPAN * BLK, kv_local, HD)
        slab_values = slab[1].reshape(SPAN * BLK, kv_local, HD)
        entries = lax.dynamic_index_in_dim(block_lists, local_blk, 0, keepdims=False)
        slab_blocks = first_blk + start_blk + jnp.arange(SPAN, dtype=jnp.int32)
        listed = jnp.any(entries[:, None] == slab_blocks[None, :], axis=0) & (slab_blocks >= 0)
        listed_tokens = jnp.repeat(listed, BLK)
        key_pos = (first_blk + start_blk) * BLK + jnp.arange(SPAN * BLK, dtype=jnp.int32)
        query_pos = position * tokens_here + local_blk * BLK + jnp.arange(BLK, dtype=jnp.int32)
        allowed = listed_tokens[None, :] & (key_pos[None, :] <= query_pos[:, None])
        scores = (
            jnp.einsum("tgqd,sgd->gqts", queries, slab_keys, preferred_element_type=jnp.float32)
            * score_scale
        )
        scores = jnp.where(allowed[None, None], scores, -1e30)
        row_max = jnp.max(scores, axis=-1, keepdims=True)
        expo = jnp.exp(scores - row_max)
        weights = (expo / jnp.sum(expo, axis=-1, keepdims=True)).astype(jnp.bfloat16)
        attended = jnp.einsum(
            "gqts,sgd->tgqd", weights, slab_values, preferred_element_type=jnp.float32
        )
        return attended.reshape(BLK, heads_local * HD)

    outputs = lax.map(one_block, jnp.arange(per_dev, dtype=jnp.int32))
    return outputs.reshape(tokens_here, heads_local * HD)


def per_device(lin_q, lin_k, lin_v, att_q, att_k, att_v, block_lists, gain_lin, gain_att):
    lin_out = linear_mixer(lin_q, lin_k, lin_v)
    att_out = tree_attention(att_q, att_k, att_v, block_lists)
    lin_squares, att_squares = lax.psum(
        (jnp.sum(lin_out * lin_out, axis=1), jnp.sum(att_out * att_out, axis=1)), "tp"
    )
    columns = lin_out.shape[1] * lax.axis_size("tp")
    lin_norm = lin_out / jnp.sqrt(lin_squares[:, None] / columns + epsilon)
    att_norm = att_out / jnp.sqrt(att_squares[:, None] / columns + epsilon)
    mixed = (
        lin_norm * gain_lin.astype(jnp.float32)[None, :]
        + att_norm * gain_att.astype(jnp.float32)[None, :]
    )
    return mixed.astype(jnp.bfloat16)


def solution(mesh):
    in_specs = (
        P("ctx", "tp"),
        P("ctx", "tp"),
        P("ctx", "tp"),
        P("ctx", "tp"),
        P("ctx", "tp"),
        P("ctx", "tp"),
        P("ctx", None),
        P("tp"),
        P("tp"),
    )
    out_specs = P("ctx", "tp")
    return jax.shard_map(
        per_device, mesh=mesh, in_specs=in_specs, out_specs=out_specs, check_vma=False
    )
```

profile of v0, /device:TPU:0, one launch (start us, length us, event | category | flops | bytes accessed | tf_op | source)
XLA Modules:
  0.0 120.2 jit_solution(1462210691689813186)
XLA Ops:
  6.5 1.1 copy.71
  7.7 0.4 copy.53
  8.1 1.1 copy.72
  9.2 1.1 fusion.34
  10.4 0.1 copy.58
  10.5 0.1 copy.59
  10.6 0.7 pad_maximum_fusion
  11.3 5.6 %collective-permute-start = (bf16[2,256,256]{1,2,0:T(8,128)(2,1)}, bf16[2,256,256]{1,2,0:T(8,128)(2,1)}, u32[]{:S(2)}, u32[]{:S(2)}) collective-permute-start(bf16[2,256,256]{1,2,0:T(8,128)(2,1)} %pad_maximum_fusion), channel_id=1, source_target_pairs={{0,8},{4,12},{8,16},{12,20},{16,24},{20,28},{1,9},{5,13},{9,17},{1... | collective-permute-start | bytes 786440 | tf_op jit(solution)/shard_map/ppermute | solution.py:30
  17.0 4.1 %collective-permute-start.1 = (bf16[2,256,256]{1,2,0:T(8,128)(2,1)}, bf16[2,256,256]{1,2,0:T(8,128)(2,1)}, u32[]{:S(2)}, u32[]{:S(2)}) collective-permute-start(bf16[2,256,256]{1,2,0:T(8,128)(2,1)} %pad_maximum_fusion), channel_id=1, source_target_pairs={{0,4},{4,8},{8,12},{12,16},{16,20},{20,24},{24,28},{1,5},{5,9},{9,... | collective-permute-start | bytes 786440 | tf_op jit(solution)/shard_map/ppermute | solution.py:30
  21.1 0.5 fusion.35
  21.6 0.8 slice.22
  22.4 1.1 copy.70
  23.7 1.6 %convolution_bitcast_fusion.1 = f32[2,128,8,128]{1,3,2,0:T(8,128)} fusion(bf16[2,128,8,128]{1,3,2,0:T(8,128)(2,1)S(1)} %copy.53, pred[128,128]{1,0:T(8,128)(4,1)S(1)} %iota_compare_fusion, bf16[2,128,8,128]{3,2,1,0:T(8,128)(2,1)S(1)} %bitcast.113, bf16[2,128,8,128]{3,2,1,0:T(8,128)(2,1)S(1)} %bitcast.114), kind=kOutput, calls=%fused_computation.32 | convolution fusion | flops 134742016 | bytes 2637824 | tf_op jit(solution)/shard_map/bhts,bshd->bthd/dot_general | solution.py:52
  25.3 6.1 %collective-permute-done.1 = bf16[2,256,256]{1,2,0:T(8,128)(2,1)} collective-permute-done((bf16[2,256,256]{1,2,0:T(8,128)(2,1)}, bf16[2,256,256]{1,2,0:T(8,128)(2,1)}, u32[]{:S(2)}, u32[]{:S(2)}) %collective-permute-start.1) | collective-permute-done | bytes 262176 | tf_op jit(solution)/shard_map/ppermute | solution.py:30
  31.4 1.1 maximum_maximum_fusion
  32.5 18.4 %while.28 = (s32[]{:T(128)}, f32[2,128,1024]{1,2,0:T(8,128)}, s32[2]{0:T(128)S(1)}, bf16[2,768,256]{1,2,0:T(8,128)(2,1)S(1)}, s32[2,4]{1,0:T(2,128)S(1)}, /*inde...) while((s32[]{:T(128)}, f32[2,128,1024]{1,2,0:T(8,128)}, ...), condition=%wide.region_10.11_spmd, body=%wide.region_6.10_spmd.sunk | while | flops 509381696 | bytes 5701822 | solution.py:104
  32.6 0.7 dynamic_slice.57
  36.0 0.1 compare_reduce_fusion.2
  36.9 0.2 compare_and_fusion.5
  37.2 1.0 constant_dynamic-slice_fusion.7
  38.2 0.2 copy.89
  38.4 1.1 fusion.58
  39.5 1.4 %fusion.59 = f32[2,128,4,128]{3,1,2,0:T(8,128)S(1)} fusion(bf16[640,2,128,1]{0,2,3,1:T(8,128)(2,1)S(1)} %bitcast.109, f32[2,4,128]{2,1,0:T(4,128)S(1)} %fusion.58, pred[128,640]{0,1:T(8,128)(4,1)S(1)} %compare_and_fusion.5, bf16[640,2,128,1]{0,2,3,1:T(8,128)(2,1)S(1)} %bitcast.108, bf16[128,2,4,128]{0,3,2,1:T(8,128)(2,1)S(1)} %bitcast.111), kind=kOutput, calls=%fused_computation.7.clone.1 | convolution fusion | flops 338822784 | bytes 1527808 | tf_op jit(solution)/shard_map/while/body/eval_jaxpr/gqts,sgd->tgqd/dot_general | solution.py:99
  40.9 0.8 constant_dynamic-update-slice_fusion.2
  41.8 0.7 dynamic_slice.57
  45.2 0.1 compare_reduce_fusion.2
  46.1 0.2 compare_and_fusion.5
  46.5 1.0 constant_dynamic-slice_fusion.7
  47.4 0.2 copy.89
  47.6 1.1 fusion.58
  48.7 1.4 %fusion.59 = f32[2,128,4,128]{3,1,2,0:T(8,128)S(1)} fusion(bf16[640,2,128,1]{0,2,3,1:T(8,128)(2,1)S(1)} %bitcast.109, f32[2,4,128]{2,1,0:T(4,128)S(1)} %fusion.58, pred[128,640]{0,1:T(8,128)(4,1)S(1)} %compare_and_fusion.5, bf16[640,2,128,1]{0,2,3,1:T(8,128)(2,1)S(1)} %bitcast.108, bf16[128,2,4,128]{0,3,2,1:T(8,128)(2,1)S(1)} %bitcast.111), kind=kOutput, calls=%fused_computation.7.clone.1 | convolution fusion | flops 338822784 | bytes 1527808 | tf_op jit(solution)/shard_map/while/body/eval_jaxpr/gqts,sgd->tgqd/dot_general | solution.py:99
  50.1 0.8 constant_dynamic-update-slice_fusion.2
  51.0 1.6 %copy.61 = f32[2,128,1024]{2,1,0:T(8,128)S(1)} copy(f32[2,128,1024]{1,2,0:T(8,128)} %get-tuple-element.247) | data formatting | bytes 2097152 | tf_op jit(solution)/shard_map/while | solution.py:104
  52.6 0.2 multiply_reduce_fusion
  52.8 39.4 %all-gather.3.cloned.1.call-done = f32[64,128,128]{2,1,0:T(8,128)} async-done(((f32[8,128,128]{2,1,0:T(8,128)}), f32[64,128,128]{2,1,0:T(8,128)}) %all-gather.3.cloned.1.call-update) | async-done | bytes 4194320 | tf_op jit(solution)/shard_map/all_gather | solution.py:16
  92.2 10.1 %while.29 = (s32[]{:T(128)}, f32[8,128,128]{2,1,0:T(8,128)S(1)}, s32[]{:T(128)}, f32[8,8,128,128]{3,2,1,0:T(8,128)}, s32[]{:T(128)}, /*index=5*/s32[]{:T(128)}) while((s32[]{:T(128)}, f32[8,128,128]{2,1,0:T(8,128)S(1)}, s32[]{:T(128)}, f32[8,8,128,128]{3,2,1,0:T(8,128)}, s32[]{:T(128)}, /*index=5*/s32[]{:T(128)}) %tuple.78), condition=%wide.region_2.3_spmd.clone, body=%wide.region_1.2_spmd.clone.sunk | while | flops 393220 | bytes 1572957 | solution.py:24
  92.2 1.3 %add_select_fusion.2 = f32[8,128,128]{2,1,0:T(8,128)S(1)} fusion(f32[8,128,128]{2,1,0:T(8,128)S(1)} %get-tuple-element.406, f32[8,8,128,128]{3,2,1,0:T(8,128)} %get-tuple-element.414, s32[]{:T(128)} %get-tuple-element.405, pred[]{:T(512)S(6)} %compare.4, pred[]{:T(512)S(6)} %lt.59), kind=kLoop, calls=%fused_computation.28.clone.1 | loop fusion | flops 393216 | bytes 1572870 | tf_op jit(solution)/shard_map/while/body/eval_jaxpr/jit(_where)/select_n | solution.py:22
  93.5 1.2 %add_select_fusion.2 = f32[8,128,128]{2,1,0:T(8,128)S(1)} fusion(f32[8,128,128]{2,1,0:T(8,128)S(1)} %get-tuple-element.406, f32[8,8,128,128]{3,2,1,0:T(8,128)} %get-tuple-element.414, s32[]{:T(128)} %get-tuple-element.405, pred[]{:T(512)S(6)} %compare.4, pred[]{:T(512)S(6)} %lt.59), kind=kLoop, calls=%fused_computation.28.clone.1 | loop fusion | flops 393216 | bytes 1572870 | tf_op jit(solution)/shard_map/while/body/eval_jaxpr/jit(_where)/select_n | solution.py:22
  94.8 1.2 %add_select_fusion.2 = f32[8,128,128]{2,1,0:T(8,128)S(1)} fusion(f32[8,128,128]{2,1,0:T(8,128)S(1)} %get-tuple-element.406, f32[8,8,128,128]{3,2,1,0:T(8,128)} %get-tuple-element.414, s32[]{:T(128)} %get-tuple-element.405, pred[]{:T(512)S(6)} %compare.4, pred[]{:T(512)S(6)} %lt.59), kind=kLoop, calls=%fused_computation.28.clone.1 | loop fusion | flops 393216 | bytes 1572870 | tf_op jit(solution)/shard_map/while/body/eval_jaxpr/jit(_where)/select_n | solution.py:22
  96.0 1.2 %add_select_fusion.2 = f32[8,128,128]{2,1,0:T(8,128)S(1)} fusion(f32[8,128,128]{2,1,0:T(8,128)S(1)} %get-tuple-element.406, f32[8,8,128,128]{3,2,1,0:T(8,128)} %get-tuple-element.414, s32[]{:T(128)} %get-tuple-element.405, pred[]{:T(512)S(6)} %compare.4, pred[]{:T(512)S(6)} %lt.59), kind=kLoop, calls=%fused_computation.28.clone.1 | loop fusion | flops 393216 | bytes 1572870 | tf_op jit(solution)/shard_map/while/body/eval_jaxpr/jit(_where)/select_n | solution.py:22
  97.3 1.2 %add_select_fusion.2 = f32[8,128,128]{2,1,0:T(8,128)S(1)} fusion(f32[8,128,128]{2,1,0:T(8,128)S(1)} %get-tuple-element.406, f32[8,8,128,128]{3,2,1,0:T(8,128)} %get-tuple-element.414, s32[]{:T(128)} %get-tuple-element.405, pred[]{:T(512)S(6)} %compare.4, pred[]{:T(512)S(6)} %lt.59), kind=kLoop, calls=%fused_computation.28.clone.1 | loop fusion | flops 393216 | bytes 1572870 | tf_op jit(solution)/shard_map/while/body/eval_jaxpr/jit(_where)/select_n | solution.py:22
  98.5 1.2 %add_select_fusion.2 = f32[8,128,128]{2,1,0:T(8,128)S(1)} fusion(f32[8,128,128]{2,1,0:T(8,128)S(1)} %get-tuple-element.406, f32[8,8,128,128]{3,2,1,0:T(8,128)} %get-tuple-element.414, s32[]{:T(128)} %get-tuple-element.405, pred[]{:T(512)S(6)} %compare.4, pred[]{:T(512)S(6)} %lt.59), kind=kLoop, calls=%fused_computation.28.clone.1 | loop fusion | flops 393216 | bytes 1572870 | tf_op jit(solution)/shard_map/while/body/eval_jaxpr/jit(_where)/select_n | solution.py:22
  99.8 1.2 %add_select_fusion.2 = f32[8,128,128]{2,1,0:T(8,128)S(1)} fusion(f32[8,128,128]{2,1,0:T(8,128)S(1)} %get-tuple-element.406, f32[8,8,128,128]{3,2,1,0:T(8,128)} %get-tuple-element.414, s32[]{:T(128)} %get-tuple-element.405, pred[]{:T(512)S(6)} %compare.4, pred[]{:T(512)S(6)} %lt.59), kind=kLoop, calls=%fused_computation.28.clone.1 | loop fusion | flops 393216 | bytes 1572870 | tf_op jit(solution)/shard_map/while/body/eval_jaxpr/jit(_where)/select_n | solution.py:22
  101.0 1.2 %add_select_fusion.2 = f32[8,128,128]{2,1,0:T(8,128)S(1)} fusion(f32[8,128,128]{2,1,0:T(8,128)S(1)} %get-tuple-element.406, f32[8,8,128,128]{3,2,1,0:T(8,128)} %get-tuple-element.414, s32[]{:T(128)} %get-tuple-element.405, pred[]{:T(512)S(6)} %compare.4, pred[]{:T(512)S(6)} %lt.59), kind=kLoop, calls=%fused_computation.28.clone.1 | loop fusion | flops 393216 | bytes 1572870 | tf_op jit(solution)/shard_map/while/body/eval_jaxpr/jit(_where)/select_n | solution.py:22
  102.3 2.6 %multiply_reduce_fusion.1 = (f32[2,128]{1,0:T(2,128)S(1)}, f32[2,128,8,128]{1,3,2,0:T(8,128)}) fusion(f32[2,128,8,128]{1,3,2,0:T(8,128)S(1)} %copy-done.1, bf16[2,128,8,128]{3,2,1,0:T(8,128)(2,1)S(1)} %bitcast.115, f32[1,8,128,128]{3,2,1,0:T(8,128)} %slice.22, f32[8,128,128]{2,1,0:T(8,128)S(1)} %get-tuple-element.246), kind=kOutput, calls=%fused_computation.41 | convolution fusion | flops 68419328 | bytes 3671040 | tf_op jit(solution)/shard_map/bthd,bhde->bthe/dot_general | solution.py:56
  104.8 1.6 %copy.57 = f32[2,128,8,128]{3,2,1,0:T(8,128)S(1)} copy(f32[2,128,8,128]{1,3,2,0:T(8,128)} %get-tuple-element.318) | data formatting | bytes 2097152 | tf_op jit(solution)/shard_map/add | solution.py:57
  106.4 5.7 %all-reduce.1 = (f32[256]{0:T(256)S(1)}, f32[256]{0:T(256)S(1)}) all-reduce(f32[256]{0:T(256)S(1)} %bitcast.126, f32[256]{0:T(256)S(1)} %bitcast.127), channel_id=1, replica_groups=mesh['ctx'=8,'tp'=4] {'tp'}, use_global_device_ids=true, to_apply=%region_12.13 | all-reduce | flops 512 | bytes 4096 | tf_op jit(solution)/shard_map/psum | solution.py:111
  112.1 1.3 %fusion.20 = bf16[256,1024]{1,0:T(8,128)(2,1)} fusion(f32[32,8,8,128]{3,2,1,0:T(8,128)S(1)} %bitcast.116, f32[2,128,1024]{2,1,0:T(8,128)S(1)} %copy.61, f32[1024]{0:T(1024)S(1)} %convert_element_type.27, f32[256]{0:T(256)S(1)} %get-tuple-element.319, f32[1024]{0:T(1024)S(1)} %convert_element_type.26, f32[256]{0:T(256)S(1)} %get-tuple-element.320), kind=kLoop, calls=%fused_computation.37 | loop fusion | flops 1572864 | bytes 2631680 | tf_op jit(solution)/shard_map/convert_element_type | solution.py:121
  (38 shorter events, 0.4 us)
Async XLA Ops:
  6.5 85.6 %all-gather.3.cloned.1.call-start = ((), (), s32[]{:S(2)}) async-start(), calls=%async_computation | async-start | bytes 4718592 | tf_op jit(solution)/shard_map/all_gather | solution.py:16
  7.7 2.7 %copy-start.2 = (bf16[256,256]{1,0:T(8,128)(2,1)S(1)}, bf16[256,256]{1,0:T(8,128)(2,1)}, u32[]{:S(2)}) copy-start(bf16[256,256]{1,0:T(8,128)(2,1)} %param.17) | copy-start | bytes 393220
  7.7 2.8 %copy-start.3 = (bf16[256,256]{1,0:T(8,128)(2,1)S(1)}, bf16[256,256]{1,0:T(8,128)(2,1)}, u32[]{:S(2)}) copy-start(bf16[256,256]{1,0:T(8,128)(2,1)} %param.18) | copy-start | bytes 393220
  10.4 13.2 %copy-start.4 = (bf16[1024]{0:T(1024)(128)(2,1)S(1)}, bf16[1024]{0:T(1024)(128)(2,1)}, u32[]{:S(2)}) copy-start(bf16[1024]{0:T(1024)(128)(2,1)} %param.20) | copy-start | bytes 6148
  10.4 13.2 %copy-start.5 = (bf16[1024]{0:T(1024)(128)(2,1)S(1)}, bf16[1024]{0:T(1024)(128)(2,1)}, u32[]{:S(2)}) copy-start(bf16[1024]{0:T(1024)(128)(2,1)} %param.21) | copy-start | bytes 6148
  11.3 14.0 %collective-permute-start = (bf16[2,256,256]{1,2,0:T(8,128)(2,1)}, bf16[2,256,256]{1,2,0:T(8,128)(2,1)}, u32[]{:S(2)}, u32[]{:S(2)}) collective-permute-start(bf16[2,256,256]{1,2,0:T(8,128)(2,1)} %pad_maximum_fusion), channel_id=1, source_target_pairs={{0,8},{4,12},{8,16},{12,20},{16,24},{20,28},{1,9},{5,13},{9,17},{1... | collective-permute-start | bytes 786440 | tf_op jit(solution)/shard_map/ppermute | solution.py:30
  17.0 14.5 %collective-permute-start.1 = (bf16[2,256,256]{1,2,0:T(8,128)(2,1)}, bf16[2,256,256]{1,2,0:T(8,128)(2,1)}, u32[]{:S(2)}, u32[]{:S(2)}) collective-permute-start(bf16[2,256,256]{1,2,0:T(8,128)(2,1)} %pad_maximum_fusion), channel_id=1, source_target_pairs={{0,4},{4,8},{8,12},{12,16},{16,20},{20,24},{24,28},{1,5},{5,9},{9,... | collective-permute-start | bytes 786440 | tf_op jit(solution)/shard_map/ppermute | solution.py:30
  22.4 10.1 %copy-start.6 = (s32[2,4]{1,0:T(2,128)S(1)}, s32[2,4]{1,0:T(2,128)}, u32[]{:S(2)}) copy-start(s32[2,4]{1,0:T(2,128)} %param.19) | copy-start | bytes 100
  51.0 1.7 %copy-start = (f32[2,128,1024]{1,2,0:T(8,128)S(1)}, f32[2,128,1024]{1,2,0:T(8,128)}, u32[]{:S(2)}) copy-start(f32[2,128,1024]{1,2,0:T(8,128)} %get-tuple-element.247) | copy-start | bytes 3145732
  92.2 10.1 %copy-start.1 = (f32[2,128,8,128]{1,3,2,0:T(8,128)S(1)}, f32[2,128,8,128]{1,3,2,0:T(8,128)}, u32[]{:S(2)}) copy-start(f32[2,128,8,128]{1,3,2,0:T(8,128)} %convolution_bitcast_fusion.1) | copy-start | bytes 3145732
Sparse Core Ops, SparseCore 0:
  10.5 81.6 all-gather.2
where the time goes:
time: 121 us; the launch traced here: 120 us
  waiting for transfers between devices  45.5 us (38%)
  other arithmetic  14.4 us (12%)
  local copies, waits for them, and re-layouts  13.7 us (11%)
  between operations  13.6 us (11%)
  matrix products  10.3 us (9%)
  starting transfers between devices  9.74 us (8%)
  loops' own time  7.28 us (6%)
  blocking collectives  5.67 us (5%)
    all_gather x1, waiting for transfers between devices, prefix_2(): everything = lax.all_gather(x, axis)  39.4 us
    select_n x8, other arithmetic, step(): return jnp.where(reached, new, before)  9.9 us
    ppermute x2, starting transfers between devices, from_behind(): return lax.ppermute(block, axis, route)  9.73 us
    another operation x1, loops' own time, tree_attention(): outputs = lax.map(one_block, jnp.arange(per_dev, dtype=jnp.int32))  7.11 us
    ppermute x2, waiting for transfers between devices, from_behind(): return lax.ppermute(block, axis, route)  6.14 us
    psum x1, blocking collectives, per_device(): lax.psum((jnp.sum(lin_out * lin_out, axis=1), jnp.sum(att_out * att_out,...  5.67 us
    unnamed x19, local copies, waits for them, and re-layouts  3.65 us
    dot_general x2, matrix products, one_block(): jnp.einsum('gqts,sgd->tgqd', weights, slab_values, preferred_element_type...  2.84 us
  transfers between devices with their start and end apart: 3, of which 2 were waited for; matrix products, arithmetic and copies ran while one was open for 16% of the time, Pallas kernels for 0%

commit v1 on v0

v1 whole, which is shorter than its diff:
```python
import functools
import math

import jax
import jax.numpy as jnp
from jax import lax
from jax.experimental import pallas as pl
from jax.experimental.pallas import tpu as pltpu
from jax.sharding import PartitionSpec as P

HD = 128
BLK = 128
SPAN = 5
EPS = 1e-06
NEG = -1e30
MESH = pl.DeviceIdType.MESH
BF16, F32 = jnp.bfloat16, jnp.float32

SIDE = BF16
CHAIN = F32
BACK = BF16


def dot(a, b, dims):
    return lax.dot_general(a, b, (dims, ((), ())), preferred_element_type=F32)


def kernel(
    n, nt, lists, lin_q_h, lin_k_h, lin_v_h, att_q_h, att_k_h, att_v_h, gains, out,
    lin_q, lin_k, lin_v, att_q, att_k, att_v, kv, total, first, scores, lin_out, att_out,
    xout, xin, zout, zin, bout, bin_, sq_out, sq_in,
    lsem, kvs, kvr, xs, xr, zs, zr, bs, br, ns, nr,
):
    ctx, tp = lax.axis_index("ctx"), lax.axis_index("tp")
    p, o = lax.rem(ctx, 2), lax.div(ctx, 2)
    mate = ctx + 1 - 2 * p
    tokens = lin_q.shape[0]
    heads = lin_q.shape[1] // HD
    kv_heads = att_k.shape[1] // HD
    half = heads // 2
    has_prev, has_next = o > 0, o < n // 2 - 1
    side, ahead, behind = {"ctx": mate}, {"ctx": ctx + 2}, {"ctx": ctx - 2}

    pairs = (
        (lin_k_h, lin_k), (lin_v_h, lin_v), (lin_q_h, lin_q),
        (att_q_h, att_q), (att_k_h, att_k), (att_v_h, att_v),
    )
    local = [pltpu.make_async_copy(s, d, lsem.at[i]) for i, (s, d) in enumerate(pairs)]
    for c in local:
        c.start()

    barrier = pltpu.get_barrier_semaphore()

    def greet(where):
        pl.semaphore_signal(barrier, inc=1, device_id=where, device_id_type=MESH)

    greet(side)
    for k in range(1, nt):
        greet({"tp": lax.rem(tp + k, nt)})
    pl.when(has_prev)(lambda: greet(behind))
    pl.when(has_next)(lambda: greet(ahead))
    pl.semaphore_wait(barrier, nt + has_prev.astype(jnp.int32) + has_next.astype(jnp.int32))

    def remote(src, dst, ssem, rsem, where):
        return pltpu.make_async_remote_copy(
            src_ref=src, dst_ref=dst, send_sem=ssem, recv_sem=rsem,
            device_id=where, device_id_type=MESH,
        )

    kv_src = (att_k_h, att_v_h)
    kv_ahead = [remote(kv_src[a], kv.at[1, a], kvs.at[a], kvr.at[a], ahead) for a in range(2)]
    kv_side = [remote(kv_src[a], kv.at[0, a], kvs.at[2 + a], kvr.at[2 + a], side) for a in range(2)]
    kv_pass = [remote(kv.at[1, a], kv.at[0, a], kvs.at[2 + a], kvr.at[2 + a], side) for a in range(2)]
    for a in range(2):
        pl.when(has_next)(kv_ahead[a].start)
        pl.when(p == 0)(kv_side[a].start)

    @pl.when(jnp.logical_not(has_prev))
    def _():
        kv[1] = jnp.zeros_like(kv[1])

        @pl.when(p == 0)
        def _():
            kv[0] = jnp.zeros_like(kv[0])

    local[0].wait()
    local[1].wait()

    def lanes(h):
        return pl.ds(pl.multiple_of(h * HD, HD), HD)

    x_copy = [remote(xout.at[j], xin.at[j], xs.at[j], xr.at[j], side) for j in range(half)]
    z_copy = [remote(zout.at[j], zin.at[j], zs.at[j], zr.at[j], ahead) for j in range(half)]
    b_copy = [remote(bout.at[j], bin_.at[j], bs.at[j], br.at[j], side) for j in range(half)]
    other, mine = (1 - p) * half, p * half

    for j in range(half):
        h = other + j
        xout[j] = dot(lin_k[:, lanes(h)], lin_v[:, lanes(h)], ((0,), (0,))).astype(SIDE)
        x_copy[j].start()
    for j in range(half):
        h = mine + j
        total[j] = dot(lin_k[:, lanes(h)], lin_v[:, lanes(h)], ((0,), (0,)))

    local[2].wait()
    row = lax.broadcasted_iota(jnp.int32, (BLK, BLK), 0)
    col = lax.broadcasted_iota(jnp.int32, (BLK, BLK), 1)
    lower = row >= col
    blocks = tokens // BLK
    for h in range(heads):
        hs = pl.ds(h * HD, HD)
        for b in range(blocks):
            rows = pl.ds(b * BLK, BLK)
            s = dot(lin_q[rows, hs], lin_k[rows, hs], ((1,), (1,)))
            scores[rows, hs] = jnp.where(lower, s, 0.0).astype(BF16)
        first[h] = dot(lin_k[0:BLK, hs], lin_v[0:BLK, hs], ((0,), (0,)))

    for a in range(2):
        @pl.when(has_prev)
        def _():
            kv_ahead[a].wait_recv()

            @pl.when(p == 1)
            def _():
                kv_pass[a].start()

    for j in range(half):
        @pl.when(has_prev)
        def _():
            z_copy[j].wait_recv()

        @pl.when(jnp.logical_not(has_prev))
        def _():
            zin[j] = jnp.zeros_like(zin[j])

        x_copy[j].wait_recv()
        before = zin[j].astype(F32)
        here, there = total[j], xin[j].astype(F32)
        zout[j] = (before + here + there).astype(CHAIN)
        pl.when(has_next)(z_copy[j].start)
        bout[j] = jnp.where(p == 0, before + here, before).astype(BACK)
        b_copy[j].start()
        total[j] = jnp.where(p == 0, before, before + there)

    for c in local[3:]:
        c.wait()
    for a in range(2):
        @pl.when((p == 1) | has_prev)
        def _():
            kv_side[a].wait_recv()

    factor = (HD ** -0.5) * math.log2(math.e)
    att_sq = [None] * blocks
    for b in range(blocks):
        rows = pl.ds(b * BLK, BLK)
        block = ctx * blocks + b
        bias = []
        for i in range(SPAN - 1):
            key_block = block - (SPAN - 1) + i
            hit = lists[b, 0] == key_block
            for e in range(1, 4):
                hit = hit | (lists[b, e] == key_block)
            bias.append(jnp.where(hit & (key_block >= 0), 0.0, NEG).astype(F32))
        bias_row = jnp.concatenate([jnp.full((1, BLK), v, F32) for v in bias], axis=1)

        def window(a, own, hs):
            parts = [kv[1, a, b * BLK:, hs], kv[0, a, :, hs], own[: (b + 1) * BLK, hs]]
            return jnp.concatenate(parts, axis=0)

        for g in range(kv_heads):
            gs = pl.ds(g * HD, HD)
            keys, values = window(0, att_k, gs), window(1, att_v, gs)
            for h in range(g * heads // kv_heads, (g + 1) * heads // kv_heads):
                hs = pl.ds(h * HD, HD)
                s = dot(att_q[rows, hs], keys, ((1,), (1,)))
                cut = (SPAN - 1) * BLK
                s = jnp.concatenate(
                    [s[:, :cut] + bias_row, jnp.where(lower, s[:, cut:], NEG)], axis=1
                )
                e = jnp.exp2((s - jnp.max(s, axis=1, keepdims=True)) * factor)
                w = (e * (1.0 / jnp.sum(e, axis=1, keepdims=True))).astype(BF16)
                r = dot(w, values, ((1,), (0,)))
                att_out[rows, hs] = r
                att_sq[b] = r * r if att_sq[b] is None else att_sq[b] + r * r

    lin_sq = [None] * blocks

    def finish(h, prefix):
        for b in range(blocks):
            rows = pl.ds(b * BLK, BLK)
            low = (prefix if b == 0 else prefix + first[h]).astype(BF16)
            lhs = jnp.concatenate([scores[rows, lanes(h)], lin_q[rows, lanes(h)]], axis=1)
            rhs = jnp.concatenate([lin_v[rows, lanes(h)], low], axis=0)
            r = dot(lhs, rhs, ((1,), (0,)))
            lin_out[rows, lanes(h)] = r
            lin_sq[b] = r * r if lin_sq[b] is None else lin_sq[b] + r * r

    for j in range(half):
        finish(mine + j, total[j])
    for j in range(half):
        b_copy[j].wait_recv()
        finish(other + j, bin_[j].astype(F32))

    def as_row(parts):
        return jnp.sum(jnp.concatenate(parts, axis=0).T, axis=0, keepdims=True)

    top = lax.broadcasted_iota(jnp.int32, (8, tokens), 0) == 0
    sums = jnp.where(top, as_row(lin_sq), as_row(att_sq))
    sq_out[...] = sums
    n_copy = [
        remote(sq_out, sq_in.at[k - 1], ns.at[k - 1], nr.at[k - 1], {"tp": lax.rem(tp + k, nt)})
        for k in range(1, nt)
    ]
    for c in n_copy:
        c.start()
    for a in range(2):
        pl.when(has_next)(kv_ahead[a].wait_send)
        pl.when((p == 0) | has_prev)(kv_side[a].wait_send)
    for j in range(half):
        x_copy[j].wait_send()
        pl.when(has_next)(z_copy[j].wait_send)
        b_copy[j].wait_send()
    for k in range(nt - 1):
        n_copy[k].wait_recv()
        sums = sums + sq_in[k]
    inv = lax.rsqrt(sums * (1.0 / (nt * heads * HD)) + EPS)

    def as_column(r):
        return jnp.broadcast_to(r, (HD, tokens)).T

    lin_inv, att_inv = as_column(inv[0:1]), as_column(inv[1:2])
    for h in range(heads):
        hs = pl.ds(h * HD, HD)
        out[:, hs] = (
            lin_out[:, hs] * lin_inv * gains[0:1, hs] + att_out[:, hs] * att_inv * gains[1:2, hs]
        ).astype(BF16)
    for c in n_copy:
        c.wait_send()


def per_device(n, nt, lin_q, lin_k, lin_v, att_q, att_k, att_v, block_lists, gain_lin, gain_att):
    tokens, columns = lin_q.shape
    heads, half = columns // HD, columns // HD // 2
    gains = jnp.stack([gain_lin, gain_att]).astype(F32)
    anywhere = pl.BlockSpec(memory_space=pl.ANY)
    vmem = pl.BlockSpec(memory_space=pltpu.VMEM)
    wide, kv_wide = (tokens, columns), att_k.shape
    state = (half, HD, HD)
    dma = pltpu.SemaphoreType.DMA
    return pl.pallas_call(
        functools.partial(kernel, n, nt),
        out_shape=jax.ShapeDtypeStruct(wide, BF16),
        in_specs=[pl.BlockSpec(memory_space=pltpu.SMEM)] + [anywhere] * 6 + [vmem],
        out_specs=vmem,
        scratch_shapes=[
            pltpu.VMEM(wide, BF16), pltpu.VMEM(wide, BF16), pltpu.VMEM(wide, BF16),
            pltpu.VMEM(wide, BF16), pltpu.VMEM(kv_wide, BF16), pltpu.VMEM(kv_wide, BF16),
            pltpu.VMEM((2, 2) + kv_wide, BF16),
            pltpu.VMEM(state, F32), pltpu.VMEM((heads, HD, HD), F32),
            pltpu.VMEM(wide, BF16), pltpu.VMEM(wide, F32), pltpu.VMEM(wide, F32),
            pltpu.VMEM(state, SIDE), pltpu.VMEM(state, SIDE),
            pltpu.VMEM(state, CHAIN), pltpu.VMEM(state, CHAIN),
            pltpu.VMEM(state, BACK), pltpu.VMEM(state, BACK),
            pltpu.VMEM((8, tokens), F32), pltpu.VMEM((nt - 1, 8, tokens), F32),
            dma((6,)), dma((4,)), dma((4,)),
            dma((half,)), dma((half,)), dma((half,)), dma((half,)), dma((half,)), dma((half,)),
            dma((nt - 1,)), dma((nt - 1,)),
        ],
        compiler_params=pltpu.CompilerParams(
            collective_id=0, has_side_effects=True, vmem_limit_bytes=48 * 2 ** 20
        ),
    )(block_lists, lin_q, lin_k, lin_v, att_q, att_k, att_v, gains)


def solution(mesh):
    wide = P("ctx", "tp")
    return jax.shard_map(
        functools.partial(per_device, mesh.shape["ctx"], mesh.shape["tp"]),
        mesh=mesh,
        in_specs=(wide,) * 6 + (P("ctx", None), P("tp"), P("tp")),
        out_specs=wide,
        check_vma=False,
    )
```

time: 121 us -> 42.1 us (0.35)
  the two profiles are of different devices: /device:TPU:0 before, /device:TPU:31 now
where the time goes in v1:
time: 42.1 us; the launch traced here: 41.7 us
  Pallas kernels  33.5 us (80%)
  local copies, waits for them, and re-layouts  8.13 us (19%)
    pallas_call x1, Pallas kernels, per_device(): pl.pallas_call(functools.partial(kernel, n, nt), out_shape=jax.ShapeDtype...  33.5 us
    unnamed x17, local copies, waits for them, and re-layouts  7.42 us

profile of v1, /device:TPU:31, one launch (start us, length us, event | category | flops | bytes accessed | tf_op | source)
XLA Modules:
  0.0 41.7 jit_solution(10153484049962317268)
XLA Ops:
  0.0 0.0 copy-start.7
  0.0 0.7 %stack.9 = bf16[1,1024]{1,0:T(2,128)(2,1)S(1)} reshape(bf16[1024]{0:T(1024)(128)(2,1)} %param.16) | data formatting | bytes 4096 | tf_op jit(solution)/shard_map/stack | solution.py:244
  0.7 0.0 copy-done.7
  0.7 0.0 copy-start.6
  0.7 0.6 %copy-done.6 = s32[2,4]{1,0:T(2,128)S(1)} copy-done((s32[2,4]{1,0:T(2,128)S(1)}, s32[2,4]{1,0:T(2,128)}, u32[]{:S(2)}) %copy-start.6) | copy-done | bytes 56
  1.4 0.0 copy-start
  1.4 1.0 %copy-done = bf16[256,1024]{1,0:T(8,128)(2,1)S(1)} copy-done((bf16[256,1024]{1,0:T(8,128)(2,1)S(1)}, bf16[256,1024]{1,0:T(8,128)(2,1)}, u32[]{:S(2)}) %copy-start) | copy-done | bytes 524312
  2.4 0.0 copy-start.1
  2.4 1.0 %copy-done.1 = bf16[256,1024]{1,0:T(8,128)(2,1)S(1)} copy-done((bf16[256,1024]{1,0:T(8,128)(2,1)S(1)}, bf16[256,1024]{1,0:T(8,128)(2,1)}, u32[]{:S(2)}) %copy-start.1) | copy-done | bytes 524312
  3.5 0.0 copy-start.2
  3.5 1.0 %copy-done.2 = bf16[256,1024]{1,0:T(8,128)(2,1)S(1)} copy-done((bf16[256,1024]{1,0:T(8,128)(2,1)S(1)}, bf16[256,1024]{1,0:T(8,128)(2,1)}, u32[]{:S(2)}) %copy-start.2) | copy-done | bytes 524312
  4.5 0.0 copy-start.3
  4.5 1.0 %copy-done.3 = bf16[256,1024]{1,0:T(8,128)(2,1)S(1)} copy-done((bf16[256,1024]{1,0:T(8,128)(2,1)S(1)}, bf16[256,1024]{1,0:T(8,128)(2,1)}, u32[]{:S(2)}) %copy-start.3) | copy-done | bytes 524312
  5.6 0.0 copy-start.4
  5.6 0.9 %copy-done.4 = bf16[256,256]{1,0:T(8,128)(2,1)S(1)} copy-done((bf16[256,256]{1,0:T(8,128)(2,1)S(1)}, bf16[256,256]{1,0:T(8,128)(2,1)}, u32[]{:S(2)}) %copy-start.4) | copy-done | bytes 131096
  6.5 0.0 copy-start.5
  6.5 0.9 %copy-done.5 = bf16[256,256]{1,0:T(8,128)(2,1)S(1)} copy-done((bf16[256,256]{1,0:T(8,128)(2,1)S(1)}, bf16[256,256]{1,0:T(8,128)(2,1)}, u32[]{:S(2)}) %copy-start.5) | copy-done | bytes 131096
  7.4 33.5 %shard_map.91 = bf16[256,1024]{1,0:T(8,128)(2,1)S(1)} custom-call(s32[2,4]{1,0:T(2,128)S(1)} %copy-done.6, bf16[256,1024]{1,0:T(8,128)(2,1)S(1)} %copy-done, bf16[256,1024]{1,0:T(8,128)(2,1)S(1)} %copy-done.1, bf16[256,1024]{1,0:T(8,128)(2,1)S(1)} %copy-done.2, bf16[256,1024]{1,0:T(8,128)(2,1)S(1)} %copy-done.3, bf16[256,256]{1,0:T(8,128)(2,1)S(1)} %copy-done.4, ...), custom_call_target="tpu_custom_call" | custom-call | tf_op jit(solution)/shard_map/pallas_call | solution.py:250
  40.9 0.8 %copy.11 = bf16[256,1024]{1,0:T(8,128)(2,1)} copy(bf16[256,1024]{1,0:T(8,128)(2,1)S(1)} %shard_map.91) | data formatting | bytes 1048576
  (2 shorter events, 0.0 us)
Async XLA Ops:
  0.0 0.7 %copy-start.7 = (bf16[1024]{0:T(1024)(128)(2,1)S(1)}, bf16[1024]{0:T(1024)(128)(2,1)}, u32[]{:S(2)}) copy-start(bf16[1024]{0:T(1024)(128)(2,1)} %param.17) | copy-start | bytes 6148
  0.7 0.7 %copy-start.6 = (s32[2,4]{1,0:T(2,128)S(1)}, s32[2,4]{1,0:T(2,128)}, u32[]{:S(2)}) copy-start(s32[2,4]{1,0:T(2,128)} %lists.1) | copy-start | bytes 100
  1.4 1.0 %copy-start = (bf16[256,1024]{1,0:T(8,128)(2,1)S(1)}, bf16[256,1024]{1,0:T(8,128)(2,1)}, u32[]{:S(2)}) copy-start(bf16[256,1024]{1,0:T(8,128)(2,1)} %lin_q_h.1) | copy-start | bytes 1572868
  2.4 1.0 %copy-start.1 = (bf16[256,1024]{1,0:T(8,128)(2,1)S(1)}, bf16[256,1024]{1,0:T(8,128)(2,1)}, u32[]{:S(2)}) copy-start(bf16[256,1024]{1,0:T(8,128)(2,1)} %lin_k_h.1) | copy-start | bytes 1572868
  3.5 1.0 %copy-start.2 = (bf16[256,1024]{1,0:T(8,128)(2,1)S(1)}, bf16[256,1024]{1,0:T(8,128)(2,1)}, u32[]{:S(2)}) copy-start(bf16[256,1024]{1,0:T(8,128)(2,1)} %lin_v_h.1) | copy-start | bytes 1572868
  4.5 1.0 %copy-start.3 = (bf16[256,1024]{1,0:T(8,128)(2,1)S(1)}, bf16[256,1024]{1,0:T(8,128)(2,1)}, u32[]{:S(2)}) copy-start(bf16[256,1024]{1,0:T(8,128)(2,1)} %att_q_h.1) | copy-start | bytes 1572868
  5.6 0.9 %copy-start.4 = (bf16[256,256]{1,0:T(8,128)(2,1)S(1)}, bf16[256,256]{1,0:T(8,128)(2,1)}, u32[]{:S(2)}) copy-start(bf16[256,256]{1,0:T(8,128)(2,1)} %att_k_h.1) | copy-start | bytes 393220
  6.5 0.9 %copy-start.5 = (bf16[256,256]{1,0:T(8,128)(2,1)S(1)}, bf16[256,256]{1,0:T(8,128)(2,1)}, u32[]{:S(2)}) copy-start(bf16[256,256]{1,0:T(8,128)(2,1)} %att_v_h.1) | copy-start | bytes 393220

commit v2 on v1

--- a/solution.py
+++ b/solution.py
@@ -17,7 +17,7 @@
 BF16, F32 = jnp.bfloat16, jnp.float32
 
 SIDE = BF16
-CHAIN = F32
+CHAIN = BF16
 BACK = BF16
 
 
@@ -26,8 +26,8 @@
 
 
 def kernel(
-    n, nt, lists, lin_q_h, lin_k_h, lin_v_h, att_q_h, att_k_h, att_v_h, gains, out,
-    lin_q, lin_k, lin_v, att_q, att_k, att_v, kv, total, first, scores, lin_out, att_out,
+    n, nt, lists, lin_q_h, lin_k_h, lin_v_h, att_q_h, att_k_h, att_v_h, gain_lin_h, gain_att_h,
+    out, lin_q, lin_k, lin_v, att_q, att_k, att_v, gain_lin, gain_att, kv, total, first, scores, lin_out, att_out,
     xout, xin, zout, zin, bout, bin_, sq_out, sq_in,
     lsem, kvs, kvr, xs, xr, zs, zr, bs, br, ns, nr,
 ):
@@ -44,6 +44,7 @@
     pairs = (
         (lin_k_h, lin_k), (lin_v_h, lin_v), (lin_q_h, lin_q),
         (att_q_h, att_q), (att_k_h, att_k), (att_v_h, att_v),
+        (gain_lin_h, gain_lin), (gain_att_h, gain_att),
     )
     local = [pltpu.make_async_copy(s, d, lsem.at[i]) for i, (s, d) in enumerate(pairs)]
     for c in local:
@@ -67,13 +68,34 @@
             device_id=where, device_id_type=MESH,
         )
 
+    def kv_copies(src, slot, sem, where):
+        return [
+            [
+                remote(
+                    src[a].at[:, pl.ds(g * HD, HD)], kv.at[slot, a, :, pl.ds(g * HD, HD)],
+                    kvs.at[sem, g, a], kvr.at[sem, g, a], where,
+                )
+                for a in range(2)
+            ]
+            for g in range(kv_heads)
+        ]
+
     kv_src = (att_k_h, att_v_h)
-    kv_ahead = [remote(kv_src[a], kv.at[1, a], kvs.at[a], kvr.at[a], ahead) for a in range(2)]
-    kv_side = [remote(kv_src[a], kv.at[0, a], kvs.at[2 + a], kvr.at[2 + a], side) for a in range(2)]
-    kv_pass = [remote(kv.at[1, a], kv.at[0, a], kvs.at[2 + a], kvr.at[2 + a], side) for a in range(2)]
-    for a in range(2):
-        pl.when(has_next)(kv_ahead[a].start)
-        pl.when(p == 0)(kv_side[a].start)
+    kv_ahead = kv_copies(kv_src, 1, 1, ahead)
+    kv_side = kv_copies(kv_src, 0, 0, side)
+    kv_pass = kv_copies((kv.at[1, 0], kv.at[1, 1]), 0, 0, side)
+
+    def send_kv(g):
+        for a in range(2):
+            pl.when(has_next)(kv_ahead[g][a].start)
+            pl.when(p == 0)(kv_side[g][a].start)
+
+    def sent_kv(g):
+        for a in range(2):
+            pl.when(has_next)(kv_ahead[g][a].wait_send)
+            pl.when(p == 0)(kv_side[g][a].wait_send)
+
+    send_kv(0)
 
     @pl.when(jnp.logical_not(has_prev))
     def _():
@@ -98,6 +120,9 @@
         h = other + j
         xout[j] = dot(lin_k[:, lanes(h)], lin_v[:, lanes(h)], ((0,), (0,))).astype(SIDE)
         x_copy[j].start()
+    for g in range(1, kv_heads):
+        sent_kv(g - 1)
+        send_kv(g)
     for j in range(half):
         h = mine + j
         total[j] = dot(lin_k[:, lanes(h)], lin_v[:, lanes(h)], ((0,), (0,)))
@@ -115,67 +140,79 @@
             scores[rows, hs] = jnp.where(lower, s, 0.0).astype(BF16)
         first[h] = dot(lin_k[0:BLK, hs], lin_v[0:BLK, hs], ((0,), (0,)))
 
-    for a in range(2):
+    def forward(g):
         @pl.when(has_prev)
         def _():
-            kv_ahead[a].wait_recv()
-
-            @pl.when(p == 1)
+            for a in range(2):
+                kv_ahead[g][a].wait_recv()
+
+                @pl.when(p == 1)
+                def _():
+                    kv_pass[g][a].start()
+
+    def chain():
+        for j in range(half):
+            @pl.when(has_prev)
             def _():
-                kv_pass[a].start()
-
-    for j in range(half):
-        @pl.when(has_prev)
-        def _():
-            z_copy[j].wait_recv()
-
-        @pl.when(jnp.logical_not(has_prev))
-        def _():
-            zin[j] = jnp.zeros_like(zin[j])
-
-        x_copy[j].wait_recv()
-        before = zin[j].astype(F32)
-        here, there = total[j], xin[j].astype(F32)
-        zout[j] = (before + here + there).astype(CHAIN)
-        pl.when(has_next)(z_copy[j].start)
-        bout[j] = jnp.where(p == 0, before + here, before).astype(BACK)
-        b_copy[j].start()
-        total[j] = jnp.where(p == 0, before, before + there)
-
+                z_copy[j].wait_recv()
+
+            @pl.when(jnp.logical_not(has_prev))
+            def _():
+                zin[j] = jnp.zeros_like(zin[j])
+
+            x_copy[j].wait_recv()
+            before = zin[j].astype(F32)
+            here, there = total[j], xin[j].astype(F32)
+            zout[j] = (before + here + there).astype(CHAIN)
+            pl.when(has_next)(z_copy[j].start)
+            bout[j] = jnp.where(p == 0, before + here, before).astype(BACK)
+            b_copy[j].start()
+            total[j] = jnp.where(p == 0, before, before + there)
+
+    for g in range(kv_heads):
+        forward(g)
+    early = has_next & (o < 2)
+    middle = has_next & (o >= 2)
+    late = jnp.logical_not(has_next)
+    pl.when(early)(chain)
     for c in local[3:]:
         c.wait()
-    for a in range(2):
-        @pl.when((p == 1) | has_prev)
-        def _():
-            kv_side[a].wait_recv()
-
     factor = (HD ** -0.5) * math.log2(math.e)
-    att_sq = [None] * blocks
+    cut = (SPAN - 1) * BLK
+    bias = []
     for b in range(blocks):
-        rows = pl.ds(b * BLK, BLK)
-        block = ctx * blocks + b
-        bias = []
+        parts = []
         for i in range(SPAN - 1):
-            key_block = block - (SPAN - 1) + i
+            key_block = ctx * blocks + b - (SPAN - 1) + i
             hit = lists[b, 0] == key_block
             for e in range(1, 4):
                 hit = hit | (lists[b, e] == key_block)
-            bias.append(jnp.where(hit & (key_block >= 0), 0.0, NEG).astype(F32))
-        bias_row = jnp.concatenate([jnp.full((1, BLK), v, F32) for v in bias], axis=1)
-
-        def window(a, own, hs):
-            parts = [kv[1, a, b * BLK:, hs], kv[0, a, :, hs], own[: (b + 1) * BLK, hs]]
-            return jnp.concatenate(parts, axis=0)
-
-        for g in range(kv_heads):
-            gs = pl.ds(g * HD, HD)
-            keys, values = window(0, att_k, gs), window(1, att_v, gs)
+            value = jnp.where(hit & (key_block >= 0), 0.0, NEG).astype(F32)
+            parts.append(jnp.full((1, BLK), value, F32))
+        bias.append(jnp.concatenate(parts, axis=1))
+
+    att_sq = [None] * blocks
+
+    def attend(g):
+        gs = pl.ds(g * HD, HD)
+        for a in range(2):
+            @pl.when((p == 1) | has_prev)
+            def _():
+                kv_side[g][a].wait_recv()
+
+        for b in range(blocks):
+            rows = pl.ds(b * BLK, BLK)
+
+            def window(a, own):
+                parts = [kv[1, a, b * BLK:, gs], kv[0, a, :, gs], own[: (b + 1) * BLK, gs]]
+                return jnp.concatenate(parts, axis=0)
+
+            keys, values = window(0, att_k), window(1, att_v)
             for h in range(g * heads // kv_heads, (g + 1) * heads // kv_heads):
                 hs = pl.ds(h * HD, HD)
                 s = dot(att_q[rows, hs], keys, ((1,), (1,)))
-                cut = (SPAN - 1) * BLK
                 s = jnp.concatenate(
-                    [s[:, :cut] + bias_row, jnp.where(lower, s[:, cut:], NEG)], axis=1
+                    [s[:, :cut] + bias[b], jnp.where(lower, s[:, cut:], NEG)], axis=1
                 )
                 e = jnp.exp2((s - jnp.max(s, axis=1, keepdims=True)) * factor)
                 w = (e * (1.0 / jnp.sum(e, axis=1, keepdims=True))).astype(BF16)
@@ -183,6 +220,11 @@
                 att_out[rows, hs] = r
                 att_sq[b] = r * r if att_sq[b] is None else att_sq[b] + r * r
 
+    for g in range(kv_heads):
+        attend(g)
+        if g == 0:
+            pl.when(middle)(chain)
+    pl.when(late)(chain)
     lin_sq = [None] * blocks
 
     def finish(h, prefix):
@@ -213,9 +255,12 @@
     ]
     for c in n_copy:
         c.start()
-    for a in range(2):
-        pl.when(has_next)(kv_ahead[a].wait_send)
-        pl.when((p == 0) | has_prev)(kv_side[a].wait_send)
+    sent_kv(kv_heads - 1)
+    @pl.when((p == 1) & has_prev)
+    def _():
+        for g in range(kv_heads):
+            for a in range(2):
+                kv_pass[g][a].wait_send()
     for j in range(half):
         x_copy[j].wait_send()
         pl.when(has_next)(z_copy[j].wait_send)
@@ -232,7 +277,7 @@
     for h in range(heads):
         hs = pl.ds(h * HD, HD)
         out[:, hs] = (
-            lin_out[:, hs] * lin_inv * gains[0:1, hs] + att_out[:, hs] * att_inv * gains[1:2, hs]
+            lin_out[:, hs] * lin_inv * gain_lin[:, hs].astype(F32) + att_out[:, hs] * att_inv * gain_att[:, hs].astype(F32)
         ).astype(BF16)
     for c in n_copy:
         c.wait_send()
@@ -241,20 +286,20 @@
 def per_device(n, nt, lin_q, lin_k, lin_v, att_q, att_k, att_v, block_lists, gain_lin, gain_att):
     tokens, columns = lin_q.shape
     heads, half = columns // HD, columns // HD // 2
-    gains = jnp.stack([gain_lin, gain_att]).astype(F32)
+    gain_lin, gain_att = gain_lin.reshape(1, columns), gain_att.reshape(1, columns)
     anywhere = pl.BlockSpec(memory_space=pl.ANY)
-    vmem = pl.BlockSpec(memory_space=pltpu.VMEM)
     wide, kv_wide = (tokens, columns), att_k.shape
-    state = (half, HD, HD)
+    state, kv_heads = (half, HD, HD), kv_wide[1] // HD
     dma = pltpu.SemaphoreType.DMA
     return pl.pallas_call(
         functools.partial(kernel, n, nt),
         out_shape=jax.ShapeDtypeStruct(wide, BF16),
-        in_specs=[pl.BlockSpec(memory_space=pltpu.SMEM)] + [anywhere] * 6 + [vmem],
-        out_specs=vmem,
+        in_specs=[pl.BlockSpec(memory_space=pltpu.SMEM)] + [anywhere] * 8,
+        out_specs=pl.BlockSpec(memory_space=pltpu.VMEM),
         scratch_shapes=[
             pltpu.VMEM(wide, BF16), pltpu.VMEM(wide, BF16), pltpu.VMEM(wide, BF16),
             pltpu.VMEM(wide, BF16), pltpu.VMEM(kv_wide, BF16), pltpu.VMEM(kv_wide, BF16),
+            pltpu.VMEM((1, columns), BF16), pltpu.VMEM((1, columns), BF16),
             pltpu.VMEM((2, 2) + kv_wide, BF16),
             pltpu.VMEM(state, F32), pltpu.VMEM((heads, HD, HD), F32),
             pltpu.VMEM(wide, BF16), pltpu.VMEM(wide, F32), pltpu.VMEM(wide, F32),
@@ -262,14 +307,14 @@
             pltpu.VMEM(state, CHAIN), pltpu.VMEM(state, CHAIN),
             pltpu.VMEM(state, BACK), pltpu.VMEM(state, BACK),
             pltpu.VMEM((8, tokens), F32), pltpu.VMEM((nt - 1, 8, tokens), F32),
-            dma((6,)), dma((4,)), dma((4,)),
+            dma((8,)), dma((2, kv_heads, 2)), dma((2, kv_heads, 2)),
             dma((half,)), dma((half,)), dma((half,)), dma((half,)), dma((half,)), dma((half,)),
             dma((nt - 1,)), dma((nt - 1,)),
         ],
         compiler_params=pltpu.CompilerParams(
-            collective_id=0, has_side_effects=True, vmem_limit_bytes=48 * 2 ** 20
+            collective_id=0, has_side_effects=True, vmem_limit_bytes=63 * 2 ** 20
         ),
-    )(block_lists, lin_q, lin_k, lin_v, att_q, att_k, att_v, gains)
+    )(block_lists, lin_q, lin_k, lin_v, att_q, att_k, att_v, gain_lin, gain_att)
 
 
 def solution(mesh):

time: 42.1 us -> 30.6 us (0.73)
  the two profiles are of different devices: /device:TPU:31 before, /device:TPU:27 now
where the time goes in v2:
time: 30.6 us; the launch traced here: 30.4 us
  Pallas kernels  26.6 us (87%)
  local copies, waits for them, and re-layouts  3.75 us (12%)
    pallas_call x1, Pallas kernels, per_device(): pl.pallas_call(functools.partial(kernel, n, nt), out_shape=jax.ShapeDtype...  26.6 us
    unnamed x3, local copies, waits for them, and re-layouts  1.87 us
    reshape x1, local copies, waits for them, and re-layouts, per_device(): gain_lin.reshape(1, columns)  1.29 us

profile of v2, /device:TPU:27, one launch (start us, length us, event | category | flops | bytes accessed | tf_op | source)
XLA Modules:
  0.0 30.4 jit_solution(756406581621463489)
XLA Ops:
  0.0 0.0 copy-start
  0.0 1.3 %reshape.6.gain_lin_h = bf16[1,1024]{1,0:T(2,128)(2,1)} reshape(bf16[1024]{0:T(1024)(128)(2,1)} %param.16) | data formatting | bytes 4096 | tf_op jit(solution)/shard_map/reshape | solution.py:289
  1.3 0.0 copy-done
  1.3 0.6 %reshape.7.gain_att_h = bf16[1,1024]{1,0:T(2,128)(2,1)} reshape(bf16[1024]{0:T(1024)(128)(2,1)S(1)} %copy-done) | data formatting | bytes 4096 | tf_op jit(solution)/shard_map/reshape | solution.py:289
  1.9 26.6 %shard_map.91 = bf16[256,1024]{1,0:T(8,128)(2,1)} custom-call(s32[2,4]{1,0:T(2,128)} %lists.1, bf16[256,1024]{1,0:T(8,128)(2,1)} %lin_q_h.1, bf16[256,1024]{1,0:T(8,128)(2,1)} %lin_k_h.1, bf16[256,1024]{1,0:T(8,128)(2,1)} %lin_v_h.1, bf16[256,1024]{1,0:T(8,128)(2,1)} %att_q_h.1, bf16[256,256]{1,0:T(8,128)(2,1)} %att_k_h.1, bf16[256,256]{1,0:T(8,128)(2,1)} %att_v_h.1, ...), custom_call_target="tpu_custom_call" | custom-call | tf_op jit(solution)/shard_map/pallas_call | solution.py:294
  28.5 1.9 %copy.11 = bf16[256,1024]{1,0:T(8,128)(2,1)} copy(bf16[256,1024]{1,0:T(8,128)(2,1)} %shard_map.91) | data formatting | bytes 1048576
Async XLA Ops:
  0.0 1.3 %copy-start = (bf16[1024]{0:T(1024)(128)(2,1)S(1)}, bf16[1024]{0:T(1024)(128)(2,1)}, u32[]{:S(2)}) copy-start(bf16[1024]{0:T(1024)(128)(2,1)} %param.17) | copy-start | bytes 6148

commit v3 on v2

--- a/solution.py
+++ b/solution.py
@@ -208,16 +208,21 @@
                 return jnp.concatenate(parts, axis=0)
 
             keys, values = window(0, att_k), window(1, att_v)
-            for h in range(g * heads // kv_heads, (g + 1) * heads // kv_heads):
-                hs = pl.ds(h * HD, HD)
-                s = dot(att_q[rows, hs], keys, ((1,), (1,)))
+            group = range(g * heads // kv_heads, (g + 1) * heads // kv_heads)
+            queries = jnp.concatenate([att_q[rows, pl.ds(h * HD, HD)] for h in group], axis=0)
+            sall = dot(queries, keys, ((1,), (1,)))
+            wall = []
+            for i in range(len(group)):
+                s = sall[i * BLK:(i + 1) * BLK]
                 s = jnp.concatenate(
                     [s[:, :cut] + bias[b], jnp.where(lower, s[:, cut:], NEG)], axis=1
                 )
                 e = jnp.exp2((s - jnp.max(s, axis=1, keepdims=True)) * factor)
-                w = (e * (1.0 / jnp.sum(e, axis=1, keepdims=True))).astype(BF16)
-                r = dot(w, values, ((1,), (0,)))
-                att_out[rows, hs] = r
+                wall.append((e * (1.0 / jnp.sum(e, axis=1, keepdims=True))).astype(BF16))
+            rall = dot(jnp.concatenate(wall, axis=0), values, ((1,), (0,)))
+            for i, h in enumerate(group):
+                r = rall[i * BLK:(i + 1) * BLK]
+                att_out[rows, pl.ds(h * HD, HD)] = r
                 att_sq[b] = r * r if att_sq[b] is None else att_sq[b] + r * r
 
     for g in range(kv_heads):
@@ -274,10 +279,11 @@
         return jnp.broadcast_to(r, (HD, tokens)).T
 
     lin_inv, att_inv = as_column(inv[0:1]), as_column(inv[1:2])
+    gl, ga = gain_lin[...].astype(F32), gain_att[...].astype(F32)
     for h in range(heads):
         hs = pl.ds(h * HD, HD)
         out[:, hs] = (
-            lin_out[:, hs] * lin_inv * gain_lin[:, hs].astype(F32) + att_out[:, hs] * att_inv * gain_att[:, hs].astype(F32)
+            lin_out[:, hs] * lin_inv * gl[h:h + 1] + att_out[:, hs] * att_inv * ga[h:h + 1]
         ).astype(BF16)
     for c in n_copy:
         c.wait_send()
@@ -286,7 +292,7 @@
 def per_device(n, nt, lin_q, lin_k, lin_v, att_q, att_k, att_v, block_lists, gain_lin, gain_att):
     tokens, columns = lin_q.shape
     heads, half = columns // HD, columns // HD // 2
-    gain_lin, gain_att = gain_lin.reshape(1, columns), gain_att.reshape(1, columns)
+    gain_lin, gain_att = gain_lin.reshape(heads, HD), gain_att.reshape(heads, HD)
     anywhere = pl.BlockSpec(memory_space=pl.ANY)
     wide, kv_wide = (tokens, columns), att_k.shape
     state, kv_heads = (half, HD, HD), kv_wide[1] // HD
@@ -299,7 +305,7 @@
         scratch_shapes=[
             pltpu.VMEM(wide, BF16), pltpu.VMEM(wide, BF16), pltpu.VMEM(wide, BF16),
             pltpu.VMEM(wide, BF16), pltpu.VMEM(kv_wide, BF16), pltpu.VMEM(kv_wide, BF16),
-            pltpu.VMEM((1, columns), BF16), pltpu.VMEM((1, columns), BF16),
+            pltpu.VMEM((heads, HD), BF16), pltpu.VMEM((heads, HD), BF16),
             pltpu.VMEM((2, 2) + kv_wide, BF16),
             pltpu.VMEM(state, F32), pltpu.VMEM((heads, HD, HD), F32),
             pltpu.VMEM(wide, BF16), pltpu.VMEM(wide, F32), pltpu.VMEM(wide, F32),

time: 30.6 us -> 28.1 us (0.918)
  the two profiles are of different devices: /device:TPU:27 before, /device:TPU:25 now
where the time goes in v3:
time: 28.1 us; the launch traced here: 27.9 us
  Pallas kernels  26 us (93%)
  local copies, waits for them, and re-layouts  1.87 us (7%)
    pallas_call x1, Pallas kernels, per_device(): pl.pallas_call(functools.partial(kernel, n, nt), out_shape=jax.ShapeDtype...  26 us
    unnamed x1, local copies, waits for them, and re-layouts  1.87 us

profile of v3, /device:TPU:25, one launch (start us, length us, event | category | flops | bytes accessed | tf_op | source)
XLA Modules:
  0.0 27.9 jit_solution(3459379565273105323)
XLA Ops:
  0.0 26.0 %shard_map.91 = bf16[256,1024]{1,0:T(8,128)(2,1)} custom-call(s32[2,4]{1,0:T(2,128)} %lists.1, bf16[256,1024]{1,0:T(8,128)(2,1)} %lin_q_h.1, bf16[256,1024]{1,0:T(8,128)(2,1)} %lin_k_h.1, bf16[256,1024]{1,0:T(8,128)(2,1)} %lin_v_h.1, bf16[256,1024]{1,0:T(8,128)(2,1)} %att_q_h.1, bf16[256,256]{1,0:T(8,128)(2,1)} %att_k_h.1, bf16[256,256]{1,0:T(8,128)(2,1)} %att_v_h.1, ...), custom_call_target="tpu_custom_call" | custom-call | tf_op jit(solution)/shard_map/pallas_call | solution.py:300
  26.0 1.9 %copy.11 = bf16[256,1024]{1,0:T(8,128)(2,1)} copy(bf16[256,1024]{1,0:T(8,128)(2,1)} %shard_map.91) | data formatting | bytes 1048576

commit v4 on v3

--- a/solution.py
+++ b/solution.py
@@ -299,7 +299,7 @@
     dma = pltpu.SemaphoreType.DMA
     return pl.pallas_call(
         functools.partial(kernel, n, nt),
-        out_shape=jax.ShapeDtypeStruct(wide, BF16),
+        out_shape=pltpu.VMEM(wide, BF16),
         in_specs=[pl.BlockSpec(memory_space=pltpu.SMEM)] + [anywhere] * 8,
         out_specs=pl.BlockSpec(memory_space=pltpu.VMEM),
         scratch_shapes=[

time: 28.1 us -> 26.2 us (0.932)
  local copies, waits for them, and re-layouts: 1.87 us -> 0.8 us
  Pallas kernels: 26 us -> 25.2 us
    unnamed x1, local copies, waits for them, and re-layouts: 1.87 us -> 0.8 us
    pallas_call x1, Pallas kernels: 26 us -> 25.2 us  [per_device(): pl.pallas_call(functools.partial(kernel, n, nt), out_shape=pltpu.VMEM(wid...]
where the time goes in v4:
time: 26.2 us; the launch traced here: 26 us
  Pallas kernels  25.2 us (96%)
  local copies, waits for them, and re-layouts  0.8 us (3%)
    pallas_call x1, Pallas kernels, per_device(): pl.pallas_call(functools.partial(kernel, n, nt), out_shape=pltpu.VMEM(wid...  25.2 us
    unnamed x1, local copies, waits for them, and re-layouts  0.8 us

profile of v4, /device:TPU:25, one launch (start us, length us, event | category | flops | bytes accessed | tf_op | source)
XLA Modules:
  0.0 26.0 jit_solution(3886055231662078407)
XLA Ops:
  0.0 25.2 %shard_map.91 = bf16[256,1024]{1,0:T(8,128)(2,1)S(1)} custom-call(s32[2,4]{1,0:T(2,128)} %lists.1, bf16[256,1024]{1,0:T(8,128)(2,1)} %lin_q_h.1, bf16[256,1024]{1,0:T(8,128)(2,1)} %lin_k_h.1, bf16[256,1024]{1,0:T(8,128)(2,1)} %lin_v_h.1, bf16[256,1024]{1,0:T(8,128)(2,1)} %att_q_h.1, bf16[256,256]{1,0:T(8,128)(2,1)} %att_k_h.1, bf16[256,256]{1,0:T(8,128)(2,1)} %att_v_h.1, ...), custom_call_target="tpu_custom_call" | custom-call | tf_op jit(solution)/shard_map/pallas_call | solution.py:300
  25.2 0.8 %copy.11 = bf16[256,1024]{1,0:T(8,128)(2,1)} copy(bf16[256,1024]{1,0:T(8,128)(2,1)S(1)} %shard_map.91) | data formatting | bytes 1048576
